TPU v7x, 32 devices: a whole 2x2x4 slice. The times are simulated.
32 devices in a mesh: groups: 2 (over y), blk: 4 (over z), oct: 2 (over x), sub: 2 (over core).
Axes of the slice: x: 2, y: 2, z: 4, core: 2. Of those that a mesh axis runs over, the one named last changes fastest.
Arguments:
- positions: float32 [3, 65536], P(None, ('groups', 'blk', 'oct', 'sub')), parts along dimension 1, may hold values from 0 to 320
- polarizability: float32 [65536], P(('groups', 'blk', 'oct', 'sub')), parts along dimension 0, may hold values from 0.5 to 1.5
- permanent_field: float32 [3, 65536], P(None, ('groups', 'blk', 'oct', 'sub')), parts along dimension 1, may hold values from -40 to 40
- group_id: int32 [65536], P(('groups', 'blk', 'oct', 'sub')), parts along dimension 0, may hold values from 0 to 10921, never falling along the last dimension, each value on 1 to 6 neighbouring positions
- pair_mask: int32 [512, 9], P(('groups', 'blk', 'oct', 'sub')), parts along dimension 0, may hold values from 0 to 1, as said below
Outputs:
- dipoles: float32 [3, 65536], P(None, ('groups', 'blk', 'oct', 'sub')), parts along dimension 1
- residual: float32 [3, 65536], P(None, ('groups', 'blk', 'oct', 'sub')), parts along dimension 1
There are 2 independent parts, one for each index of `groups`. A program takes and returns all parts, laid end to end along the dimension named above; each array names one. Nothing has to cross between parts.
Inputs may be any that keep to these rules, and one draw needn't show every extreme that they name: `group_id`: never falls from one atom to the next; each value names 1 to 6 consecutive atoms. pair_mask[b, 4] = 1, and pair_mask[b, 4 + o] = pair_mask[(b + o) mod 256, 4 - o].
All inputs are finite; a program needn't handle non-finite values.
Results may differ from a plain program's by a relative error of at most 0.0003.
Values sent between devices are 32-bit elements; how exact they have to be, the bound alone decides.
No kernel may reach another device: no remote copies, remote signals or barrier semaphores. Data moves between devices by JAX's collectives and lax.ppermute only.
A program may use at most 64 MiB of HBM per device.

v0:
```python
import math
import jax
import jax.numpy as jnp
import numpy as np
from jax import lax
from jax.sharding import PartitionSpec as P

BOXES_DEV = 2
BLOCK = 128
ORDER = 5
NODE_PAD = 128
ITERS = 2
side_length = 32.0
layer_gap = 2.5
thole_damp = 0.39
highest = lax.Precision.HIGHEST


def padded(cells, sides, width):
    for axis, dim in sides:
        count = lax.axis_size(axis)
        head = lax.slice_in_dim(cells, 0, width, axis=dim)
        tail = lax.slice_in_dim(cells, cells.shape[dim] - width, cells.shape[dim], axis=dim)
        cells = jnp.concatenate(
            [
                lax.ppermute(tail, axis, [(i, (i + 1) % count) for i in range(count)]),
                cells,
                lax.ppermute(head, axis, [((i + 1) % count, i) for i in range(count)]),
            ],
            axis=dim,
        )
    return cells


def wrap_image(delta, period):
    return delta - period * jnp.floor(delta / period + 0.5)


def split_size(total, limit):
    best = 1
    for factor in range(1, min(total, limit) + 1):
        if total % factor == 0:
            best = factor
    return best


def near_tiles(target, source, moments, keep_tile, length_z):
    delta_x = wrap_image(target[0][:, :, None] - source[0][:, None, :], side_length)
    delta_y = wrap_image(target[1][:, :, None] - source[1][:, None, :], side_length)
    delta_z = wrap_image(target[2][:, :, None] - source[2][:, None, :], length_z)
    keep = (keep_tile[:, None, None] > 0.5) & (target[4][:, :, None] != source[4][:, None, :])
    dist_sq = jnp.where(keep, delta_x * delta_x + delta_y * delta_y + delta_z * delta_z, 1.0)
    inv_three = lax.rsqrt(dist_sq) / dist_sq
    scaled = (
        thole_damp
        * dist_sq
        * jnp.sqrt(dist_sq)
        * lax.rsqrt(target[3][:, :, None] * source[3][:, None, :])
    )
    lam_three = -jnp.expm1(-scaled)
    lam_five = lam_three - scaled * jnp.exp(-scaled)
    coef_five = jnp.where(keep, 3.0 * lam_five * inv_three / dist_sq, 0.0)
    coef_three = jnp.where(keep, lam_three * inv_three, 0.0)
    along = (
        delta_x * moments[0][:, None, :]
        + delta_y * moments[1][:, None, :]
        + delta_z * moments[2][:, None, :]
    )
    weighted = coef_five * along
    field_x = jnp.sum(weighted * delta_x - coef_three * moments[0][:, None, :], axis=2)
    field_y = jnp.sum(weighted * delta_y - coef_three * moments[1][:, None, :], axis=2)
    field_z = jnp.sum(weighted * delta_z - coef_three * moments[2][:, None, :], axis=2)
    return jnp.stack([field_x, field_y, field_z])


def near_total(static_ext, dipole_ext, mask_rows, length_z, atom_count):
    reach = (mask_rows.shape[1] - 1) // 2
    width = reach * BLOCK
    blocks = atom_count // BLOCK
    target = static_ext[:, width : width + atom_count].reshape(5, blocks, BLOCK)
    total = jnp.zeros((3, blocks, BLOCK), static_ext.dtype)
    for offset in range(-reach, reach + 1):
        begin = (reach + offset) * BLOCK
        source = static_ext[:, begin : begin + atom_count].reshape(5, blocks, BLOCK)
        moments = dipole_ext[:, begin : begin + atom_count].reshape(3, blocks, BLOCK)
        keep_tile = mask_rows[:, reach + offset].astype(static_ext.dtype)
        total = total + near_tiles(target, source, moments, keep_tile, length_z)
    return total.reshape(3, atom_count)


def node_tables():
    count = ORDER
    roots = np.cos((2.0 * np.arange(count) + 1.0) * np.pi / (2.0 * count))
    degree = np.arange(count)
    coeff = (
        2.0 / count * np.cos(np.outer(2.0 * np.arange(count) + 1.0, degree) * np.pi / (2.0 * count))
    )
    coeff = np.where(degree[None, :] == 0, 1.0 / count, coeff)
    index = np.arange(NODE_PAD)
    live = index < count**3
    safe = np.where(live, index, 0)
    first = safe // (count * count)
    second = safe // count % count
    third = safe % count
    levels = np.arange(count)[None, :]
    pick_a = (first[:, None] == levels) * live[:, None] * 1.0
    pick_b = (second[:, None] == levels) * 1.0
    pick_c = (third[:, None] == levels) * 1.0
    node_x = 16.0 * (1.0 + roots[first])
    node_y = 16.0 * (1.0 + roots[second])
    node_t = roots[third]
    tables = [coeff, pick_a, pick_b, pick_c, node_x, node_y, node_t]
    return [jnp.asarray(item, jnp.float32) for item in tables]


def interpolation(coords, box_ids, box_height):
    coeff, pick_a, pick_b, pick_c, node_x, node_y, node_t = node_tables()
    scaled_x = coords[0] / 16.0 - 1.0
    scaled_y = coords[1] / 16.0 - 1.0
    scaled_z = (
        2.0 * (coords[2] - box_ids.astype(coords.dtype)[:, None] * box_height) / box_height - 1.0
    )

    def basis(values, picks):
        terms = [jnp.ones_like(values), values]
        for degree in range(2, ORDER):
            terms.append(2.0 * values * terms[-1] - terms[-2])
        stacked = jnp.stack(terms[:ORDER])
        smooth = jnp.einsum("kn,nba->kba", coeff, stacked, precision=highest)
        return jnp.einsum("pk,kba->pba", picks, smooth, precision=highest)

    return basis(scaled_x, pick_a) * basis(scaled_y, pick_b) * basis(scaled_z, pick_c)


def far_block(target_ids, source_ids, weights, slabs, box_height, length_z):
    coeff, pick_a, pick_b, pick_c, node_x, node_y, node_t = node_tables()
    height_t = (
        target_ids.astype(weights.dtype)[:, None] * box_height
        + 0.5 * box_height * (1.0 + node_t)[None, :]
    )
    height_s = (
        source_ids.astype(weights.dtype)[:, None] * box_height
        + 0.5 * box_height * (1.0 + node_t)[None, :]
    )
    delta_x = wrap_image(node_x[:, None] - node_x[None, :], side_length)[None, :, None, :]
    delta_y = wrap_image(node_y[:, None] - node_y[None, :], side_length)[None, :, None, :]
    delta_z = wrap_image(height_t[:, :, None, None] - height_s[None, None, :, :], length_z)
    apart = jnp.abs(target_ids[:, None] // BOXES_DEV - source_ids[None, :] // BOXES_DEV)
    apart = jnp.minimum(apart, slabs - apart)
    keep = (apart >= 1)[:, None, :, None]
    dist_sq = jnp.where(
        keep,
        delta_x * delta_x + delta_y * delta_y + delta_z * delta_z + box_height * box_height,
        1.0,
    )
    inv_three = lax.rsqrt(dist_sq) / dist_sq
    coef_five = jnp.where(keep, 3.0 * inv_three / dist_sq, 0.0)
    coef_three = jnp.where(keep, inv_three, 0.0)
    weight_x = weights[:, 0, :][None, None]
    weight_y = weights[:, 1, :][None, None]
    weight_z = weights[:, 2, :][None, None]
    weighted = coef_five * (delta_x * weight_x + delta_y * weight_y + delta_z * weight_z)
    field_x = jnp.sum(weighted * delta_x - coef_three * weight_x, axis=(2, 3))
    field_y = jnp.sum(weighted * delta_y - coef_three * weight_y, axis=(2, 3))
    field_z = jnp.sum(weighted * delta_z - coef_three * weight_z, axis=(2, 3))
    return jnp.stack([field_x, field_y, field_z], axis=1)


def on_device(positions, polarizability, permanent_field, group_id, pair_mask):
    slabs = lax.axis_size(("blk", "oct", "sub"))
    member = lax.axis_index(("blk", "oct", "sub"))
    atom_count = positions.shape[1]
    length_z = layer_gap * atom_count * slabs / 256.0
    box_height = length_z / (BOXES_DEV * slabs)
    per_box = atom_count // BOXES_DEV
    width = (pair_mask.shape[1] - 1) // 2 * BLOCK
    group_limit = max(1, 32 // BOXES_DEV)
    static = jnp.concatenate(
        [positions, polarizability[None, :], group_id.astype(jnp.float32)[None, :]], axis=0
    )
    static_ext = padded(static, ((("blk", "oct", "sub"), 1),), width)
    own_boxes = member * BOXES_DEV + jnp.arange(BOXES_DEV, dtype=jnp.int32)
    interp = interpolation(positions.reshape(3, BOXES_DEV, per_box), own_boxes, box_height)
    surface = 4.0 * math.pi / 3.0 / (side_length * side_length * length_z)

    def induced(dipoles, total):
        dipole_ext = padded(dipoles, ((("blk", "oct", "sub"), 1),), width)
        near = near_total(static_ext, dipole_ext, pair_mask, length_z, atom_count)
        weights = jnp.einsum(
            "pba,cba->bcp", interp, dipoles.reshape(3, BOXES_DEV, per_box), precision=highest
        )
        piece = lax.all_gather(weights, ("blk", "oct", "sub"), axis=0, tiled=True)
        start = jnp.int32(0)
        count = piece.shape[0]
        size = split_size(count, group_limit)
        grouped = piece.reshape(count // size, size, 3, piece.shape[2])

        def visit(acc, item):
            index, bundle = item
            sources = start + index * size + jnp.arange(size, dtype=jnp.int32)
            return (acc + far_block(own_boxes, sources, bundle, slabs, box_height, length_z), None)

        result, unused = lax.scan(
            visit, jnp.zeros_like(weights), (jnp.arange(count // size, dtype=jnp.int32), grouped)
        )
        far = jnp.einsum("pba,bcp->cba", interp, result, precision=highest).reshape(3, atom_count)
        return near + far - surface * total[:, None]

    def moment(values):
        return lax.psum(jnp.sum(values, axis=1), ("blk", "oct", "sub"))

    def squares(resid, scaled):
        return lax.psum(jnp.sum(resid * scaled), ("blk", "oct", "sub"))

    dipoles = polarizability[None, :] * permanent_field
    residual = induced(dipoles, moment(dipoles))
    precond = polarizability[None, :] * residual
    direction = precond
    norm_now = squares(residual, precond)
    for step in range(ITERS):
        image = direction / polarizability[None, :] - induced(direction, moment(direction))
        rate = norm_now / lax.psum(jnp.sum(direction * image), ("blk", "oct", "sub"))
        dipoles = dipoles + rate * direction
        residual = residual - rate * image
        if step + 1 < ITERS:
            precond = polarizability[None, :] * residual
            norm_next = squares(residual, precond)
            direction = precond + norm_next / norm_now * direction
            norm_now = norm_next
    return (dipoles, residual)


def solution(mesh):
    return jax.shard_map(
        on_device,
        mesh=mesh,
        in_specs=(
            P(None, ("groups", "blk", "oct", "sub")),
            P(("groups", "blk", "oct", "sub")),
            P(None, ("groups", "blk", "oct", "sub")),
            P(("groups", "blk", "oct", "sub")),
            P(("groups", "blk", "oct", "sub"), None),
        ),
        out_specs=(
            P(None, ("groups", "blk", "oct", "sub")),
            P(None, ("groups", "blk", "oct", "sub")),
        ),
        check_vma=False,
    )
```

profile of v0, /device:TPU:0, one launch (start us, length us, event | category | flops | bytes accessed | tf_op | source)
XLA Modules:
  0.0 428.3 jit_solution(15247812564218952183)
XLA Ops:
  2.6 5.0 %collective-permute-start.2 = (f32[5,512]{1,0:T(8,128)S(1)}, f32[5,512]{1,0:T(8,128)S(1)}, u32[]{:S(2)}, u32[]{:S(2)}) collective-permute-start(f32[5,512]{1,0:T(8,128)S(1)} %get-tuple-element.990), channel_id=1, source_target_pairs={{1,0},{2,1},{3,2},{4,3},{5,4},{6,5},{7,6},{8,7},{9,8},{10,9},{11,1... | collective-permute-start | bytes 30728 | tf_op jit(solution)/shard_map/ppermute | solution.py:28
  14.0 29.5 %psum.49 = f32[3]{0:T(128)S(1)} all-reduce(f32[3]{0:T(128)S(1)} %get-tuple-element.927), channel_id=1, replica_groups=mesh['groups'=2,'blk'=4,'oct'=2,'sub'=2] {'blk','oct','sub'}, use_global_device_ids=true, to_apply=%region_33.34 | all-reduce | flops 3 | bytes 24 | tf_op jit(solution)/shard_map/psum | solution.py:210
  52.0 17.8 %all_gather.9 = f32[32,3,128]{2,1,0:T(4,128)S(1)} all-gather(f32[2,3,128]{2,1,0:T(4,128)S(1)} %fusion.782), channel_id=1, replica_groups=mesh['groups'=2,'blk'=4,'oct'=2,'sub'=2] {'blk','oct','sub'}, dimensions={0}, use_global_device_ids=true | all-gather | bytes 52224 | tf_op jit(solution)/shard_map/all_gather | solution.py:192
  69.9 13.5 %while.51 = (s32[]{:T(128)}, f32[2,3,128]{2,0,1:T(2,128)S(1)}, s32[2]{0:T(128)S(1)}, f32[2,16,3,128]{3,1,2,0:T(8,128)S(1)}, s32[]{:T(128)}, /*index=5*/s32[]{:T(...) while((s32[]{:T(128)}, f32[2,3,128]{2,0,1:T(2,128)S(1)}, ...), condition=%wide.region_31.32_spmd.clone.clone.clone.clone, body=%wide.region_27.31_spmd.sunk.clone.clone.clone.clone.sunk | while | flops 16765948 | bytes 2795035 | solution.py:203
  71.8 4.8 %subtract_reduce_fusion.9 = (f32[2,128]{1,0:T(2,128)S(1)}, f32[2,128]{1,0:T(2,128)S(1)}, f32[2,128]{1,0:T(2,128)S(1)}) fusion(f32[16,128]{1,0:T(8,128)S(1)} %get-tuple-element.1216, f32[128,128]{1,0:T(8,128)S(1)} %get-tuple-element.1217, pred[2,16]{1,0:T(4,128)(4,1)S(1)} %fusion.814, f32[16,128]{1,0:T(8,128)S(1)} %broadcast_add_fusion.12, ...), kind=kLoop, calls=%fused_computation.28.clone.1 | loop fusion | flops 15727872 | bytes 1282080 | tf_op jit(solution)/shard_map/while/body/eval_jaxpr/reduce_sum | solution.py:163
  78.5 4.8 %subtract_reduce_fusion.9 = (f32[2,128]{1,0:T(2,128)S(1)}, f32[2,128]{1,0:T(2,128)S(1)}, f32[2,128]{1,0:T(2,128)S(1)}) fusion(f32[16,128]{1,0:T(8,128)S(1)} %get-tuple-element.1216, f32[128,128]{1,0:T(8,128)S(1)} %get-tuple-element.1217, pred[2,16]{1,0:T(4,128)(4,1)S(1)} %fusion.814, f32[16,128]{1,0:T(8,128)S(1)} %broadcast_add_fusion.12, ...), kind=kLoop, calls=%fused_computation.28.clone.1 | loop fusion | flops 15727872 | bytes 1282080 | tf_op jit(solution)/shard_map/while/body/eval_jaxpr/reduce_sum | solution.py:163
  112.2 7.3 %fusion.630 = (f32[16,128]{1,0:T(8,128)S(1)}, f32[16,128]{1,0:T(8,128)S(1)}, f32[16,128]{1,0:T(8,128)S(1)}, f32[16,128]{1,0:T(8,128)S(1)}, f32[16,128]{1,0:T(8,128)S(1)}, /*index=5*/f32[16,128]{1,0:T(8,128)S(1)}) fusion(f32[16,128]{1,0:T(8,128)S(1)} %bitcast.840, f32[16,128]{1,0:T(8,128)S(1)} %bitcast.735, f32[16,128]{1,0:T(8,128)S(1)} %bitcast.931, ...), kind=kLoop, calls=%fused_computation.815 | loop fusion | flops 30920704 | bytes 180256 | tf_op jit(solution)/shard_map/reduce_sum | solution.py:70
  120.7 31.6 %psum.51 = f32[3]{0:T(128)S(1)} all-reduce(f32[3]{0:T(128)S(1)} %get-tuple-element.923), channel_id=1, replica_groups=mesh['groups'=2,'blk'=4,'oct'=2,'sub'=2] {'blk','oct','sub'}, use_global_device_ids=true, to_apply=%region_69.70 | all-reduce | flops 3 | bytes 24 | tf_op jit(solution)/shard_map/psum | solution.py:210
  153.2 4.4 %collective-permute-start.5 = (f32[3,512]{1,0:T(4,128)S(1)}, f32[3,512]{1,0:T(4,128)S(1)}, u32[]{:S(2)}, u32[]{:S(2)}) collective-permute-start(f32[3,512]{1,0:T(4,128)S(1)} %get-tuple-element.1078), channel_id=1, source_target_pairs={{1,0},{2,1},{3,2},{4,3},{5,4},{6,5},{7,6},{8,7},{9,8},{10,9},{11,1... | collective-permute-start | bytes 18440 | tf_op jit(solution)/shard_map/ppermute | solution.py:28
  157.6 17.3 %all_gather.10 = f32[32,3,128]{2,1,0:T(4,128)S(1)} all-gather(f32[2,3,128]{2,1,0:T(4,128)S(1)} %fusion.684), channel_id=1, replica_groups=mesh['groups'=2,'blk'=4,'oct'=2,'sub'=2] {'blk','oct','sub'}, dimensions={0}, use_global_device_ids=true | all-gather | bytes 52224 | tf_op jit(solution)/shard_map/all_gather | solution.py:192
  174.9 13.0 %while.52 = (s32[]{:T(128)}, f32[2,3,128]{2,0,1:T(2,128)S(1)}, s32[2]{0:T(128)S(1)}, f32[2,16,3,128]{3,1,2,0:T(8,128)S(1)}, s32[]{:T(128)}, /*index=5*/s32[]{:T(...) while((s32[]{:T(128)}, f32[2,3,128]{2,0,1:T(2,128)S(1)}, ...), condition=%wide.region_67.68_spmd.clone.clone.clone.clone, body=%wide.region_63.67_spmd.sunk.clone.clone.clone.clone.sunk | while | flops 16765948 | bytes 2795035 | solution.py:203
  176.6 4.8 %subtract_reduce_fusion.10 = (f32[2,128]{1,0:T(2,128)S(1)}, f32[2,128]{1,0:T(2,128)S(1)}, f32[2,128]{1,0:T(2,128)S(1)}) fusion(f32[16,128]{1,0:T(8,128)S(1)} %get-tuple-element.1230, f32[128,128]{1,0:T(8,128)S(1)} %get-tuple-element.1231, pred[2,16]{1,0:T(4,128)(4,1)S(1)} %fusion.817, f32[16,128]{1,0:T(8,128)S(1)} %broadcast_add_fusion.14, ...), kind=kLoop, calls=%fused_computation.82.clone.1 | loop fusion | flops 15727872 | bytes 1282080 | tf_op jit(solution)/shard_map/while/body/eval_jaxpr/reduce_sum | solution.py:163
  183.1 4.8 %subtract_reduce_fusion.10 = (f32[2,128]{1,0:T(2,128)S(1)}, f32[2,128]{1,0:T(2,128)S(1)}, f32[2,128]{1,0:T(2,128)S(1)}) fusion(f32[16,128]{1,0:T(8,128)S(1)} %get-tuple-element.1230, f32[128,128]{1,0:T(8,128)S(1)} %get-tuple-element.1231, pred[2,16]{1,0:T(4,128)(4,1)S(1)} %fusion.817, f32[16,128]{1,0:T(8,128)S(1)} %broadcast_add_fusion.14, ...), kind=kLoop, calls=%fused_computation.82.clone.1 | loop fusion | flops 15727872 | bytes 1282080 | tf_op jit(solution)/shard_map/while/body/eval_jaxpr/reduce_sum | solution.py:163
  216.1 7.3 %fusion.629 = (f32[16,128]{1,0:T(8,128)S(1)}, f32[16,128]{1,0:T(8,128)S(1)}, f32[16,128]{1,0:T(8,128)S(1)}, f32[16,128]{1,0:T(8,128)S(1)}, f32[16,128]{1,0:T(8,128)S(1)}, /*index=5*/f32[16,128]{1,0:T(8,128)S(1)}) fusion(f32[16,128]{1,0:T(8,128)S(1)} %bitcast.872, f32[16,128]{1,0:T(8,128)S(1)} %bitcast.736, f32[16,128]{1,0:T(8,128)S(1)} %bitcast.939, ...), kind=kLoop, calls=%fused_computation.814 | loop fusion | flops 30920704 | bytes 180256 | tf_op jit(solution)/shard_map/reduce_sum | solution.py:70
  225.1 32.1 %all-reduce = (f32[]{:T(128)}, f32[]{:T(128)}) all-reduce(f32[]{:T(128)} %get-tuple-element.870, f32[]{:T(128)} %get-tuple-element.869), channel_id=1, replica_groups=mesh['groups'=2,'blk'=4,'oct'=2,'sub'=2] {'blk','oct','sub'}, use_global_device_ids=true, to_apply=%region_35.36 | all-reduce | flops 2 | bytes 16 | tf_op jit(solution)/shard_map/psum | solution.py:213
  259.1 30.1 %psum.53 = f32[]{:T(128)} all-reduce(f32[]{:T(128)} %fusion.632), channel_id=1, replica_groups=mesh['groups'=2,'blk'=4,'oct'=2,'sub'=2] {'blk','oct','sub'}, use_global_device_ids=true, to_apply=%region_73.74 | all-reduce | flops 1 | bytes 8 | tf_op jit(solution)/shard_map/psum | solution.py:213
  290.6 29.7 %psum.54 = f32[3]{0:T(128)S(1)} all-reduce(f32[3]{0:T(128)S(1)} %get-tuple-element.918), channel_id=1, replica_groups=mesh['groups'=2,'blk'=4,'oct'=2,'sub'=2] {'blk','oct','sub'}, use_global_device_ids=true, to_apply=%region_107.108 | all-reduce | flops 3 | bytes 24 | tf_op jit(solution)/shard_map/psum | solution.py:210
  321.3 4.4 %collective-permute-start.7 = (f32[3,512]{1,0:T(4,128)S(1)}, f32[3,512]{1,0:T(4,128)S(1)}, u32[]{:S(2)}, u32[]{:S(2)}) collective-permute-start(f32[3,512]{1,0:T(4,128)S(1)} %get-tuple-element.1070), channel_id=1, source_target_pairs={{1,0},{2,1},{3,2},{4,3},{5,4},{6,5},{7,6},{8,7},{9,8},{10,9},{11,1... | collective-permute-start | bytes 18440 | tf_op jit(solution)/shard_map/ppermute | solution.py:28
  325.7 17.3 %all_gather.11 = f32[32,3,128]{2,1,0:T(4,128)S(1)} all-gather(f32[2,3,128]{2,1,0:T(4,128)S(1)} %fusion.783), channel_id=1, replica_groups=mesh['groups'=2,'blk'=4,'oct'=2,'sub'=2] {'blk','oct','sub'}, dimensions={0}, use_global_device_ids=true | all-gather | bytes 52224 | tf_op jit(solution)/shard_map/all_gather | solution.py:192
  343.0 13.0 %while.53 = (s32[]{:T(128)}, f32[2,3,128]{2,0,1:T(2,128)S(1)}, s32[2]{0:T(128)S(1)}, f32[2,16,3,128]{3,1,2,0:T(8,128)S(1)}, s32[]{:T(128)}, /*index=5*/s32[]{:T(...) while((s32[]{:T(128)}, f32[2,3,128]{2,0,1:T(2,128)S(1)}, ...), condition=%wide.region_105.106_spmd.clone.clone.clone.clone, body=%wide.region_101.105_spmd.sunk.clone.clone.clone.clone.sunk | while | flops 16765948 | bytes 2795035 | solution.py:203
  344.7 4.8 %subtract_reduce_fusion.11 = (f32[2,128]{1,0:T(2,128)S(1)}, f32[2,128]{1,0:T(2,128)S(1)}, f32[2,128]{1,0:T(2,128)S(1)}) fusion(f32[16,128]{1,0:T(8,128)S(1)} %get-tuple-element.1244, f32[128,128]{1,0:T(8,128)S(1)} %get-tuple-element.1245, pred[2,16]{1,0:T(4,128)(4,1)S(1)} %fusion.820, f32[16,128]{1,0:T(8,128)S(1)} %broadcast_add_fusion.16, ...), kind=kLoop, calls=%fused_computation.136.clone.1 | loop fusion | flops 15727872 | bytes 1282080 | tf_op jit(solution)/shard_map/while/body/eval_jaxpr/reduce_sum | solution.py:163
  351.2 4.8 %subtract_reduce_fusion.11 = (f32[2,128]{1,0:T(2,128)S(1)}, f32[2,128]{1,0:T(2,128)S(1)}, f32[2,128]{1,0:T(2,128)S(1)}) fusion(f32[16,128]{1,0:T(8,128)S(1)} %get-tuple-element.1244, f32[128,128]{1,0:T(8,128)S(1)} %get-tuple-element.1245, pred[2,16]{1,0:T(4,128)(4,1)S(1)} %fusion.820, f32[16,128]{1,0:T(8,128)S(1)} %broadcast_add_fusion.16, ...), kind=kLoop, calls=%fused_computation.136.clone.1 | loop fusion | flops 15727872 | bytes 1282080 | tf_op jit(solution)/shard_map/while/body/eval_jaxpr/reduce_sum | solution.py:163
  384.3 7.3 %fusion.628 = (f32[16,128]{1,0:T(8,128)S(1)}, f32[16,128]{1,0:T(8,128)S(1)}, f32[16,128]{1,0:T(8,128)S(1)}, f32[16,128]{1,0:T(8,128)S(1)}, f32[16,128]{1,0:T(8,128)S(1)}, /*index=5*/f32[16,128]{1,0:T(8,128)S(1)}) fusion(f32[16,128]{1,0:T(8,128)S(1)} %bitcast.862, f32[16,128]{1,0:T(8,128)S(1)} %bitcast.737, f32[16,128]{1,0:T(8,128)S(1)} %bitcast.947, ...), kind=kLoop, calls=%fused_computation.813 | loop fusion | flops 30920704 | bytes 180256 | tf_op jit(solution)/shard_map/reduce_sum | solution.py:70
  393.2 32.0 %psum.55 = f32[]{:T(128)} all-reduce(f32[]{:T(128)} %get-tuple-element.1104), channel_id=1, replica_groups=mesh['groups'=2,'blk'=4,'oct'=2,'sub'=2] {'blk','oct','sub'}, use_global_device_ids=true, to_apply=%region_109.110 | all-reduce | flops 1 | bytes 8 | tf_op jit(solution)/shard_map/psum | solution.py:222
  (198 shorter events, 116.9 us)
Async XLA Ops:
  0.6 45.0 %copy-start.8 = (f32[5,5,1]{1,0,2:T(8,128)S(1)}, f32[5,5,1]{1,0,2:T(8,128)}, u32[]{:S(2)}) copy-start(f32[5,5,1]{1,0,2:T(8,128)} %constant.532) | copy-start | bytes 304
  0.6 45.2 %copy-start.11 = (f32[128,5,1]{0,1,2:T(8,128)S(1)}, f32[128,5,1]{0,1,2:T(8,128)}, u32[]{:S(2)}) copy-start(f32[128,5,1]{0,1,2:T(8,128)} %constant.533) | copy-start | bytes 7684
  2.1 81.8 %collective-permute-start = (f32[5,512]{1,0:T(8,128)S(1)}, f32[5,512]{1,0:T(8,128)S(1)}, u32[]{:S(2)}, u32[]{:S(2)}) collective-permute-start(f32[5,512]{1,0:T(8,128)S(1)} %get-tuple-element.989), channel_id=1, source_target_pairs={{0,1},{1,2},{2,3},{3,4},{4,5},{5,6},{6,7},{7,8},{8,9},{9,10},{10,1... | collective-permute-start | bytes 30728 | tf_op jit(solution)/shard_map/ppermute | solution.py:26
  2.6 81.3 %collective-permute-start.2 = (f32[5,512]{1,0:T(8,128)S(1)}, f32[5,512]{1,0:T(8,128)S(1)}, u32[]{:S(2)}, u32[]{:S(2)}) collective-permute-start(f32[5,512]{1,0:T(8,128)S(1)} %get-tuple-element.990), channel_id=1, source_target_pairs={{1,0},{2,1},{3,2},{4,3},{5,4},{6,5},{7,6},{8,7},{9,8},{10,9},{11,1... | collective-permute-start | bytes 30728 | tf_op jit(solution)/shard_map/ppermute | solution.py:28
  8.6 75.2 %collective-permute-start.1 = (f32[3,512]{1,0:T(4,128)S(1)}, f32[3,512]{1,0:T(4,128)S(1)}, u32[]{:S(2)}, u32[]{:S(2)}) collective-permute-start(f32[3,512]{1,0:T(4,128)S(1)} %get-tuple-element.1085), channel_id=1, source_target_pairs={{0,1},{1,2},{2,3},{3,4},{4,5},{5,6},{6,7},{7,8},{8,9},{9,10},{10,1... | collective-permute-start | bytes 18440 | tf_op jit(solution)/shard_map/ppermute | solution.py:26
  8.6 75.2 %collective-permute-start.3 = (f32[3,512]{1,0:T(4,128)S(1)}, f32[3,512]{1,0:T(4,128)S(1)}, u32[]{:S(2)}, u32[]{:S(2)}) collective-permute-start(f32[3,512]{1,0:T(4,128)S(1)} %get-tuple-element.1086), channel_id=1, source_target_pairs={{1,0},{2,1},{3,2},{4,3},{5,4},{6,5},{7,6},{8,7},{9,8},{10,9},{11,1... | collective-permute-start | bytes 18440 | tf_op jit(solution)/shard_map/ppermute | solution.py:28
  13.1 34.7 %copy-start.10 = (f32[128,5,1]{0,1,2:T(8,128)S(1)}, f32[128,5,1]{0,1,2:T(8,128)}, u32[]{:S(2)}) copy-start(f32[128,5,1]{0,1,2:T(8,128)} %constant.534) | copy-start | bytes 7684
  47.7 1.8 copy-start.9
  51.4 18.4 %copy-start.2 = (f32[128]{0:T(128)S(1)}, f32[128]{0:T(128)}, u32[]{:S(2)}) copy-start(f32[128]{0:T(128)} %constant.2011) | copy-start | bytes 1540
  51.4 18.4 %copy-start.4 = (f32[128]{0:T(128)S(1)}, f32[128]{0:T(128)}, u32[]{:S(2)}) copy-start(f32[128]{0:T(128)} %constant.489.clone..sunk.15) | copy-start | bytes 1540
  51.4 18.4 %copy-start.5 = (f32[128]{0:T(128)S(1)}, f32[128]{0:T(128)}, u32[]{:S(2)}) copy-start(f32[128]{0:T(128)} %constant.2010) | copy-start | bytes 1540
  51.4 18.4 %copy-start.6 = (f32[128]{0:T(128)S(1)}, f32[128]{0:T(128)}, u32[]{:S(2)}) copy-start(f32[128]{0:T(128)} %constant.490.clone..sunk.15) | copy-start | bytes 1540
  51.4 18.4 %copy-start.7 = (f32[128]{0:T(128)S(1)}, f32[128]{0:T(128)}, u32[]{:S(2)}) copy-start(f32[128]{0:T(128)} %constant.2009) | copy-start | bytes 1540
  69.9 13.5 %copy-start = (s32[16,9]{1,0:T(8,128)S(1)}, s32[16,9]{1,0:T(8,128)}, u32[]{:S(2)}) copy-start(s32[16,9]{1,0:T(8,128)} %param.28) | copy-start | bytes 1732
  69.9 13.8 %copy-start.1 = (f32[2048]{0:T(1024)S(1)}, f32[2048]{0:T(1024)}, u32[]{:S(2)}) copy-start(f32[2048]{0:T(1024)} %param.25) | copy-start | bytes 24580
  69.9 14.0 %copy-start.3 = (f32[3,2048]{1,0:T(4,128)S(1)}, f32[3,2048]{1,0:T(4,128)}, u32[]{:S(2)}) copy-start(f32[3,2048]{1,0:T(4,128)} %param.24) | copy-start | bytes 73732
  153.1 34.8 %collective-permute-start.4 = (f32[3,512]{1,0:T(4,128)S(1)}, f32[3,512]{1,0:T(4,128)S(1)}, u32[]{:S(2)}, u32[]{:S(2)}) collective-permute-start(f32[3,512]{1,0:T(4,128)S(1)} %get-tuple-element.1077), channel_id=1, source_target_pairs={{0,1},{1,2},{2,3},{3,4},{4,5},{5,6},{6,7},{7,8},{8,9},{9,10},{10,1... | collective-permute-start | bytes 18440 | tf_op jit(solution)/shard_map/ppermute | solution.py:26
  153.2 34.8 %collective-permute-start.5 = (f32[3,512]{1,0:T(4,128)S(1)}, f32[3,512]{1,0:T(4,128)S(1)}, u32[]{:S(2)}, u32[]{:S(2)}) collective-permute-start(f32[3,512]{1,0:T(4,128)S(1)} %get-tuple-element.1078), channel_id=1, source_target_pairs={{1,0},{2,1},{3,2},{4,3},{5,4},{6,5},{7,6},{8,7},{9,8},{10,9},{11,1... | collective-permute-start | bytes 18440 | tf_op jit(solution)/shard_map/ppermute | solution.py:28
  321.2 34.8 %collective-permute-start.6 = (f32[3,512]{1,0:T(4,128)S(1)}, f32[3,512]{1,0:T(4,128)S(1)}, u32[]{:S(2)}, u32[]{:S(2)}) collective-permute-start(f32[3,512]{1,0:T(4,128)S(1)} %get-tuple-element.1069), channel_id=1, source_target_pairs={{0,1},{1,2},{2,3},{3,4},{4,5},{5,6},{6,7},{7,8},{8,9},{9,10},{10,1... | collective-permute-start | bytes 18440 | tf_op jit(solution)/shard_map/ppermute | solution.py:26
  321.3 34.8 %collective-permute-start.7 = (f32[3,512]{1,0:T(4,128)S(1)}, f32[3,512]{1,0:T(4,128)S(1)}, u32[]{:S(2)}, u32[]{:S(2)}) collective-permute-start(f32[3,512]{1,0:T(4,128)S(1)} %get-tuple-element.1070), channel_id=1, source_target_pairs={{1,0},{2,1},{3,2},{4,3},{5,4},{6,5},{7,6},{8,7},{9,8},{10,9},{11,1... | collective-permute-start | bytes 18440 | tf_op jit(solution)/shard_map/ppermute | solution.py:28
where the time goes:
time: 434 us; the launch traced here: 428 us
  blocking collectives  237 us (55%)
  other arithmetic  145 us (33%)
  starting transfers between devices  19 us (4%)
  matrix products  13.6 us (3%)
  between operations  5.61 us (1%)
    reduce_sum x24, other arithmetic, near_tiles(): jnp.sum(weighted * delta_x - coef_three * moments[0][:, None, :], axis=2)  106 us
    psum x3, blocking collectives, moment(): return lax.psum(jnp.sum(values, axis=1), ('blk', 'oct', 'sub'))  90.8 us
    psum x2, blocking collectives, squares(): return lax.psum(jnp.sum(resid * scaled), ('blk', 'oct', 'sub'))  62.2 us
    all_gather x3, blocking collectives, induced(): piece = lax.all_gather(weights, ('blk', 'oct', 'sub'), axis=0, tiled=True)  52.3 us
    psum x1, blocking collectives, on_device(): lax.psum(jnp.sum(direction * image), ('blk', 'oct', 'sub'))  32 us
    reduce_sum x6, other arithmetic, far_block(): field_x = jnp.sum(weighted * delta_x - coef_three * weight_x, axis=(2, 3))  28.8 us
    ppermute x4, starting transfers between devices, padded(): lax.ppermute(head, axis, [((i + 1) % count, i) for i in range(count)])  18.3 us
  transfers between devices with their start and end apart: 8, of which 0 were waited for; matrix products, arithmetic and copies ran while one was open for 11% of the time, Pallas kernels for 0%

commit v1 on v0

--- a/solution.py
+++ b/solution.py
@@ -14,6 +14,24 @@
 layer_gap = 2.5
 thole_damp = 0.39
 highest = lax.Precision.HIGHEST
+
+
+def laid_out(parts, dim):
+    parts = jnp.moveaxis(parts, 0, dim)
+    lengths = parts.shape
+    return parts.reshape(*lengths[:dim], lengths[dim] * lengths[dim + 1], *lengths[dim + 2 :])
+
+
+def grow_blocks(x, axis):
+    size = lax.axis_size(axis)
+    tiles = x[None]
+    for level in range(size.bit_length() - 1):
+        distance = 1 << level
+        other = lax.ppermute(tiles, axis, [(i, i ^ distance) for i in range(size)])
+        both = jnp.stack([tiles, other])
+        upper = lax.axis_index(axis) >> level & 1
+        tiles = jnp.where(upper == 0, both, both[::-1]).reshape(-1, *x.shape)
+    return tiles
 
 
 def padded(cells, sides, width):
@@ -189,7 +207,7 @@
         weights = jnp.einsum(
             "pba,cba->bcp", interp, dipoles.reshape(3, BOXES_DEV, per_box), precision=highest
         )
-        piece = lax.all_gather(weights, ("blk", "oct", "sub"), axis=0, tiled=True)
+        piece = laid_out(grow_blocks(weights, ("blk", "oct", "sub")), 0)
         start = jnp.int32(0)
         count = piece.shape[0]
         size = split_size(count, group_limit)

time: 434 us -> 395 us (0.910)
  blocking collectives: 237 us -> 188 us
  waiting for transfers between devices: 0.02 us -> 8.03 us
    all_gather x3 -> x0, blocking collectives: 52.3 us -> none  [induced(): piece = lax.all_gather(weights, ('blk', 'oct', 'sub'), axis=0, tiled=True)]
    ppermute x0 -> x12, waiting for transfers between devices: none -> 5.48 us  [grow_blocks(): other = lax.ppermute(tiles, axis, [(i, i ^ distance) for i in range(size)])]
  transfers between devices with their start and end apart: 8 -> 20, of which waited for: 0 -> 8; matrix products, arithmetic and copies ran while one was open for 11% -> 30% of each run, Pallas kernels for 0% -> 0%
where the time goes in v1:
time: 395 us; the launch traced here: 389 us
  blocking collectives  188 us (48%)
  other arithmetic  145 us (37%)
  starting transfers between devices  20.2 us (5%)
  matrix products  13.6 us (3%)
  waiting for transfers between devices  8.03 us (2%)
  between operations  5.92 us (1%)
  local copies, waits for them, and re-layouts  4.23 us (1%)
  loops' own time  4.04 us (1%)
    reduce_sum x24, other arithmetic, near_tiles(): jnp.sum(weighted * delta_x - coef_three * moments[0][:, None, :], axis=2)  106 us
    psum x3, blocking collectives, moment(): return lax.psum(jnp.sum(values, axis=1), ('blk', 'oct', 'sub'))  90.1 us
    psum x2, blocking collectives, squares(): return lax.psum(jnp.sum(resid * scaled), ('blk', 'oct', 'sub'))  63.9 us
    psum x1, blocking collectives, on_device(): lax.psum(jnp.sum(direction * image), ('blk', 'oct', 'sub'))  33.8 us
    reduce_sum x6, other arithmetic, far_block(): field_x = jnp.sum(weighted * delta_x - coef_three * weight_x, axis=(2, 3))  28.8 us
    ppermute x4, starting transfers between devices, padded(): lax.ppermute(head, axis, [((i + 1) % count, i) for i in range(count)])  17.7 us
  transfers between devices with their start and end apart: 20, of which 8 were waited for; matrix products, arithmetic and copies ran while one was open for 30% of the time, Pallas kernels for 0%

profile of v1, /device:TPU:0, one launch (start us, length us, event | category | flops | bytes accessed | tf_op | source)
XLA Modules:
  0.0 388.7 jit_solution(8315216135176778362)
XLA Ops:
  2.6 5.0 %collective-permute-start.2 = (f32[5,512]{1,0:T(8,128)S(1)}, f32[5,512]{1,0:T(8,128)S(1)}, u32[]{:S(2)}, u32[]{:S(2)}) collective-permute-start(f32[5,512]{1,0:T(8,128)S(1)} %get-tuple-element.975), channel_id=1, source_target_pairs={{1,0},{2,1},{3,2},{4,3},{5,4},{6,5},{7,6},{8,7},{9,8},{10,9},{11,1... | collective-permute-start | bytes 30728 | tf_op jit(solution)/shard_map/ppermute | solution.py:46
  8.6 4.4 %collective-permute-start.3 = (f32[3,512]{1,0:T(4,128)S(1)}, f32[3,512]{1,0:T(4,128)S(1)}, u32[]{:S(2)}, u32[]{:S(2)}) collective-permute-start(f32[3,512]{1,0:T(4,128)S(1)} %get-tuple-element.1071), channel_id=1, source_target_pairs={{1,0},{2,1},{3,2},{4,3},{5,4},{6,5},{7,6},{8,7},{9,8},{10,9},{11,1... | collective-permute-start | bytes 18440 | tf_op jit(solution)/shard_map/ppermute | solution.py:46
  22.6 30.4 %psum.49 = f32[3]{0:T(128)S(1)} all-reduce(f32[3]{0:T(128)S(1)} %get-tuple-element.912), channel_id=1, replica_groups=mesh['groups'=2,'blk'=4,'oct'=2,'sub'=2] {'blk','oct','sub'}, use_global_device_ids=true, to_apply=%region_33.34 | all-reduce | flops 3 | bytes 24 | tf_op jit(solution)/shard_map/psum | solution.py:228
  77.6 7.3 %fusion.630 = (f32[16,128]{1,0:T(8,128)S(1)}, f32[16,128]{1,0:T(8,128)S(1)}, f32[16,128]{1,0:T(8,128)S(1)}, f32[16,128]{1,0:T(8,128)S(1)}, f32[16,128]{1,0:T(8,128)S(1)}, /*index=5*/f32[16,128]{1,0:T(8,128)S(1)}) fusion(f32[16,128]{1,0:T(8,128)S(1)} %bitcast.918, f32[16,128]{1,0:T(8,128)S(1)} %bitcast.849, f32[16,128]{1,0:T(8,128)S(1)} %bitcast.1004, ...), kind=kLoop, calls=%fused_computation.815 | loop fusion | flops 30920704 | bytes 180256 | tf_op jit(solution)/shard_map/reduce_sum | solution.py:88
  93.8 13.3 %while.51 = (s32[]{:T(128)}, f32[2,3,128]{2,0,1:T(2,128)S(1)}, s32[2]{0:T(128)S(1)}, f32[2,16,3,128]{3,1,2,0:T(8,128)S(1)}, s32[]{:T(128)}, /*index=5*/s32[]{:T(...) while((s32[]{:T(128)}, f32[2,3,128]{2,0,1:T(2,128)S(1)}, ...), condition=%wide.region_31.32_spmd.clone.clone.clone.clone, body=%wide.region_27.31_spmd.sunk.clone.clone.clone.clone.sunk | while | flops 16765948 | bytes 2795035 | solution.py:221
  95.6 4.8 %subtract_reduce_fusion.9 = (f32[2,128]{1,0:T(2,128)S(1)}, f32[2,128]{1,0:T(2,128)S(1)}, f32[2,128]{1,0:T(2,128)S(1)}) fusion(f32[16,128]{1,0:T(8,128)S(1)} %get-tuple-element.1207, f32[128,128]{1,0:T(8,128)S(1)} %get-tuple-element.1208, pred[2,16]{1,0:T(4,128)(4,1)S(1)} %fusion.820, f32[16,128]{1,0:T(8,128)S(1)} %broadcast_add_fusion.12, ...), kind=kLoop, calls=%fused_computation.28.clone.1 | loop fusion | flops 15727872 | bytes 1282080 | tf_op jit(solution)/shard_map/while/body/eval_jaxpr/reduce_sum | solution.py:181
  102.3 4.8 %subtract_reduce_fusion.9 = (f32[2,128]{1,0:T(2,128)S(1)}, f32[2,128]{1,0:T(2,128)S(1)}, f32[2,128]{1,0:T(2,128)S(1)}) fusion(f32[16,128]{1,0:T(8,128)S(1)} %get-tuple-element.1207, f32[128,128]{1,0:T(8,128)S(1)} %get-tuple-element.1208, pred[2,16]{1,0:T(4,128)(4,1)S(1)} %fusion.820, f32[16,128]{1,0:T(8,128)S(1)} %broadcast_add_fusion.12, ...), kind=kLoop, calls=%fused_computation.28.clone.1 | loop fusion | flops 15727872 | bytes 1282080 | tf_op jit(solution)/shard_map/while/body/eval_jaxpr/reduce_sum | solution.py:181
  108.2 30.2 %psum.51 = f32[3]{0:T(128)S(1)} all-reduce(f32[3]{0:T(128)S(1)} %get-tuple-element.908), channel_id=1, replica_groups=mesh['groups'=2,'blk'=4,'oct'=2,'sub'=2] {'blk','oct','sub'}, use_global_device_ids=true, to_apply=%region_69.70 | all-reduce | flops 3 | bytes 24 | tf_op jit(solution)/shard_map/psum | solution.py:228
  139.9 4.1 %collective-permute-start.9 = (f32[3,512]{1,0:T(4,128)S(1)}, f32[3,512]{1,0:T(4,128)S(1)}, u32[]{:S(2)}, u32[]{:S(2)}) collective-permute-start(f32[3,512]{1,0:T(4,128)S(1)} %get-tuple-element.1063), channel_id=1, source_target_pairs={{1,0},{2,1},{3,2},{4,3},{5,4},{6,5},{7,6},{8,7},{9,8},{10,9},{11,1... | collective-permute-start | bytes 18440 | tf_op jit(solution)/shard_map/ppermute | solution.py:46
  145.4 4.0 %fusion.602 = (f32[16,128]{1,0:T(8,128)S(1)}, f32[16,128]{1,0:T(8,128)S(1)}, f32[16,128]{1,0:T(8,128)S(1)}) fusion(f32[16,128]{1,0:T(8,128)S(1)} %bitcast.964, f32[16,128]{1,0:T(8,128)S(1)} %bitcast.907, f32[16,128]{1,0:T(8,128)S(1)} %bitcast.1007, f32[16,128]{1,0:T(8,128)S(1)} %bitcast.965, f32[16,128]{1,0:T(8,128)S(1)} %bitcast.963, ...), kind=kLoop, calls=%fused_computation.787 | loop fusion | flops 15460352 | bytes 131088 | tf_op jit(solution)/shard_map/reduce_sum | solution.py:88
  161.6 7.3 %fusion.629 = (f32[16,128]{1,0:T(8,128)S(1)}, f32[16,128]{1,0:T(8,128)S(1)}, f32[16,128]{1,0:T(8,128)S(1)}, f32[16,128]{1,0:T(8,128)S(1)}, f32[16,128]{1,0:T(8,128)S(1)}, /*index=5*/f32[16,128]{1,0:T(8,128)S(1)}) fusion(f32[16,128]{1,0:T(8,128)S(1)} %bitcast.956, f32[16,128]{1,0:T(8,128)S(1)} %bitcast.850, f32[16,128]{1,0:T(8,128)S(1)} %bitcast.1011, ...), kind=kLoop, calls=%fused_computation.814 | loop fusion | flops 30920704 | bytes 180256 | tf_op jit(solution)/shard_map/reduce_sum | solution.py:88
  181.9 13.2 %while.52 = (s32[]{:T(128)}, f32[2,3,128]{2,0,1:T(2,128)S(1)}, s32[2]{0:T(128)S(1)}, f32[2,16,3,128]{3,1,2,0:T(8,128)S(1)}, s32[]{:T(128)}, /*index=5*/s32[]{:T(...) while((s32[]{:T(128)}, f32[2,3,128]{2,0,1:T(2,128)S(1)}, ...), condition=%wide.region_67.68_spmd.clone.clone.clone.clone, body=%wide.region_63.67_spmd.sunk.clone.clone.clone.clone.sunk | while | flops 16765948 | bytes 2795035 | solution.py:221
  183.7 4.8 %subtract_reduce_fusion.10 = (f32[2,128]{1,0:T(2,128)S(1)}, f32[2,128]{1,0:T(2,128)S(1)}, f32[2,128]{1,0:T(2,128)S(1)}) fusion(f32[16,128]{1,0:T(8,128)S(1)} %get-tuple-element.1221, f32[128,128]{1,0:T(8,128)S(1)} %get-tuple-element.1222, pred[2,16]{1,0:T(4,128)(4,1)S(1)} %fusion.823, f32[16,128]{1,0:T(8,128)S(1)} %broadcast_add_fusion.14, ...), kind=kLoop, calls=%fused_computation.82.clone.1 | loop fusion | flops 15727872 | bytes 1282080 | tf_op jit(solution)/shard_map/while/body/eval_jaxpr/reduce_sum | solution.py:181
  190.3 4.8 %subtract_reduce_fusion.10 = (f32[2,128]{1,0:T(2,128)S(1)}, f32[2,128]{1,0:T(2,128)S(1)}, f32[2,128]{1,0:T(2,128)S(1)}) fusion(f32[16,128]{1,0:T(8,128)S(1)} %get-tuple-element.1221, f32[128,128]{1,0:T(8,128)S(1)} %get-tuple-element.1222, pred[2,16]{1,0:T(4,128)(4,1)S(1)} %fusion.823, f32[16,128]{1,0:T(8,128)S(1)} %broadcast_add_fusion.14, ...), kind=kLoop, calls=%fused_computation.82.clone.1 | loop fusion | flops 15727872 | bytes 1282080 | tf_op jit(solution)/shard_map/while/body/eval_jaxpr/reduce_sum | solution.py:181
  196.8 33.8 %all-reduce = (f32[]{:T(128)}, f32[]{:T(128)}) all-reduce(f32[]{:T(128)} %get-tuple-element.855, f32[]{:T(128)} %get-tuple-element.854), channel_id=1, replica_groups=mesh['groups'=2,'blk'=4,'oct'=2,'sub'=2] {'blk','oct','sub'}, use_global_device_ids=true, to_apply=%region_35.36 | all-reduce | flops 2 | bytes 16 | tf_op jit(solution)/shard_map/psum | solution.py:231
  232.6 30.1 %psum.53 = f32[]{:T(128)} all-reduce(f32[]{:T(128)} %fusion.632), channel_id=1, replica_groups=mesh['groups'=2,'blk'=4,'oct'=2,'sub'=2] {'blk','oct','sub'}, use_global_device_ids=true, to_apply=%region_73.74 | all-reduce | flops 1 | bytes 8 | tf_op jit(solution)/shard_map/psum | solution.py:231
  264.1 29.5 %psum.54 = f32[3]{0:T(128)S(1)} all-reduce(f32[3]{0:T(128)S(1)} %get-tuple-element.903), channel_id=1, replica_groups=mesh['groups'=2,'blk'=4,'oct'=2,'sub'=2] {'blk','oct','sub'}, use_global_device_ids=true, to_apply=%region_107.108 | all-reduce | flops 3 | bytes 24 | tf_op jit(solution)/shard_map/psum | solution.py:228
  295.1 4.2 %collective-permute-start.15 = (f32[3,512]{1,0:T(4,128)S(1)}, f32[3,512]{1,0:T(4,128)S(1)}, u32[]{:S(2)}, u32[]{:S(2)}) collective-permute-start(f32[3,512]{1,0:T(4,128)S(1)} %get-tuple-element.1055), channel_id=1, source_target_pairs={{1,0},{2,1},{3,2},{4,3},{5,4},{6,5},{7,6},{8,7},{9,8},{10,9},{11,1... | collective-permute-start | bytes 18440 | tf_op jit(solution)/shard_map/ppermute | solution.py:46
  304.7 4.0 %fusion.601 = (f32[16,128]{1,0:T(8,128)S(1)}, f32[16,128]{1,0:T(8,128)S(1)}, f32[16,128]{1,0:T(8,128)S(1)}) fusion(f32[16,128]{1,0:T(8,128)S(1)} %bitcast.950, f32[16,128]{1,0:T(8,128)S(1)} %bitcast.908, f32[16,128]{1,0:T(8,128)S(1)} %bitcast.1016, f32[16,128]{1,0:T(8,128)S(1)} %bitcast.951, f32[16,128]{1,0:T(8,128)S(1)} %bitcast.949, ...), kind=kLoop, calls=%fused_computation.786 | loop fusion | flops 15460352 | bytes 131088 | tf_op jit(solution)/shard_map/reduce_sum | solution.py:88
  316.8 7.3 %fusion.628 = (f32[16,128]{1,0:T(8,128)S(1)}, f32[16,128]{1,0:T(8,128)S(1)}, f32[16,128]{1,0:T(8,128)S(1)}, f32[16,128]{1,0:T(8,128)S(1)}, f32[16,128]{1,0:T(8,128)S(1)}, /*index=5*/f32[16,128]{1,0:T(8,128)S(1)}) fusion(f32[16,128]{1,0:T(8,128)S(1)} %bitcast.952, f32[16,128]{1,0:T(8,128)S(1)} %bitcast.851, f32[16,128]{1,0:T(8,128)S(1)} %bitcast.1019, ...), kind=kLoop, calls=%fused_computation.813 | loop fusion | flops 30920704 | bytes 180256 | tf_op jit(solution)/shard_map/reduce_sum | solution.py:88
  337.2 13.0 %while.53 = (s32[]{:T(128)}, f32[2,3,128]{2,0,1:T(2,128)S(1)}, s32[2]{0:T(128)S(1)}, f32[2,16,3,128]{3,1,2,0:T(8,128)S(1)}, s32[]{:T(128)}, /*index=5*/s32[]{:T(...) while((s32[]{:T(128)}, f32[2,3,128]{2,0,1:T(2,128)S(1)}, ...), condition=%wide.region_105.106_spmd.clone.clone.clone.clone, body=%wide.region_101.105_spmd.sunk.clone.clone.clone.clone.sunk | while | flops 16765948 | bytes 2795035 | solution.py:221
  338.9 4.8 %subtract_reduce_fusion.11 = (f32[2,128]{1,0:T(2,128)S(1)}, f32[2,128]{1,0:T(2,128)S(1)}, f32[2,128]{1,0:T(2,128)S(1)}) fusion(f32[16,128]{1,0:T(8,128)S(1)} %get-tuple-element.1235, f32[128,128]{1,0:T(8,128)S(1)} %get-tuple-element.1236, pred[2,16]{1,0:T(4,128)(4,1)S(1)} %fusion.826, f32[16,128]{1,0:T(8,128)S(1)} %broadcast_add_fusion.16, ...), kind=kLoop, calls=%fused_computation.136.clone.1 | loop fusion | flops 15727872 | bytes 1282080 | tf_op jit(solution)/shard_map/while/body/eval_jaxpr/reduce_sum | solution.py:181
  345.4 4.8 %subtract_reduce_fusion.11 = (f32[2,128]{1,0:T(2,128)S(1)}, f32[2,128]{1,0:T(2,128)S(1)}, f32[2,128]{1,0:T(2,128)S(1)}) fusion(f32[16,128]{1,0:T(8,128)S(1)} %get-tuple-element.1235, f32[128,128]{1,0:T(8,128)S(1)} %get-tuple-element.1236, pred[2,16]{1,0:T(4,128)(4,1)S(1)} %fusion.826, f32[16,128]{1,0:T(8,128)S(1)} %broadcast_add_fusion.16, ...), kind=kLoop, calls=%fused_computation.136.clone.1 | loop fusion | flops 15727872 | bytes 1282080 | tf_op jit(solution)/shard_map/while/body/eval_jaxpr/reduce_sum | solution.py:181
  351.9 33.8 %psum.55 = f32[]{:T(128)} all-reduce(f32[]{:T(128)} %get-tuple-element.1095), channel_id=1, replica_groups=mesh['groups'=2,'blk'=4,'oct'=2,'sub'=2] {'blk','oct','sub'}, use_global_device_ids=true, to_apply=%region_109.110 | all-reduce | flops 1 | bytes 8 | tf_op jit(solution)/shard_map/psum | solution.py:240
  (246 shorter events, 114.5 us)
Async XLA Ops:
  0.6 15.8 %copy-start.11 = (f32[128,5,1]{0,1,2:T(8,128)S(1)}, f32[128,5,1]{0,1,2:T(8,128)}, u32[]{:S(2)}) copy-start(f32[128,5,1]{0,1,2:T(8,128)} %constant.537) | copy-start | bytes 7684
  2.1 55.1 %collective-permute-start = (f32[5,512]{1,0:T(8,128)S(1)}, f32[5,512]{1,0:T(8,128)S(1)}, u32[]{:S(2)}, u32[]{:S(2)}) collective-permute-start(f32[5,512]{1,0:T(8,128)S(1)} %get-tuple-element.974), channel_id=1, source_target_pairs={{0,1},{1,2},{2,3},{3,4},{4,5},{5,6},{6,7},{7,8},{8,9},{9,10},{10,1... | collective-permute-start | bytes 30728 | tf_op jit(solution)/shard_map/ppermute | solution.py:44
  2.6 54.6 %collective-permute-start.2 = (f32[5,512]{1,0:T(8,128)S(1)}, f32[5,512]{1,0:T(8,128)S(1)}, u32[]{:S(2)}, u32[]{:S(2)}) collective-permute-start(f32[5,512]{1,0:T(8,128)S(1)} %get-tuple-element.975), channel_id=1, source_target_pairs={{1,0},{2,1},{3,2},{4,3},{5,4},{6,5},{7,6},{8,7},{9,8},{10,9},{11,1... | collective-permute-start | bytes 30728 | tf_op jit(solution)/shard_map/ppermute | solution.py:46
  8.6 44.9 %collective-permute-start.1 = (f32[3,512]{1,0:T(4,128)S(1)}, f32[3,512]{1,0:T(4,128)S(1)}, u32[]{:S(2)}, u32[]{:S(2)}) collective-permute-start(f32[3,512]{1,0:T(4,128)S(1)} %get-tuple-element.1070), channel_id=1, source_target_pairs={{0,1},{1,2},{2,3},{3,4},{4,5},{5,6},{6,7},{7,8},{8,9},{9,10},{10,1... | collective-permute-start | bytes 18440 | tf_op jit(solution)/shard_map/ppermute | solution.py:44
  8.6 44.9 %collective-permute-start.3 = (f32[3,512]{1,0:T(4,128)S(1)}, f32[3,512]{1,0:T(4,128)S(1)}, u32[]{:S(2)}, u32[]{:S(2)}) collective-permute-start(f32[3,512]{1,0:T(4,128)S(1)} %get-tuple-element.1071), channel_id=1, source_target_pairs={{1,0},{2,1},{3,2},{4,3},{5,4},{6,5},{7,6},{8,7},{9,8},{10,9},{11,1... | collective-permute-start | bytes 18440 | tf_op jit(solution)/shard_map/ppermute | solution.py:46
  21.9 31.1 %copy-start = (s32[16,9]{1,0:T(8,128)S(1)}, s32[16,9]{1,0:T(8,128)}, u32[]{:S(2)}) copy-start(s32[16,9]{1,0:T(8,128)} %param.28) | copy-start | bytes 1732
  21.9 31.5 %copy-start.1 = (f32[2048]{0:T(1024)S(1)}, f32[2048]{0:T(1024)}, u32[]{:S(2)}) copy-start(f32[2048]{0:T(1024)} %param.25) | copy-start | bytes 24580
  21.9 35.3 %copy-start.3 = (f32[3,2048]{1,0:T(4,128)S(1)}, f32[3,2048]{1,0:T(4,128)}, u32[]{:S(2)}) copy-start(f32[3,2048]{1,0:T(4,128)} %param.24) | copy-start | bytes 73732
  22.5 30.9 %collective-permute-start.4 = (f32[1,2,3,128]{3,2,1,0:T(4,128)S(1)}, f32[1,2,3,128]{3,2,1,0:T(4,128)S(1)}, u32[]{:S(2)}, u32[]{:S(2)}) collective-permute-start(f32[1,2,3,128]{3,2,1,0:T(4,128)S(1)} %bitcast.766), channel_id=1, source_target_pairs={{0,1},{1,0},{2,3},{3,2},{4,5},{5,4},{6,7},{7,6},{8,9},{9,8},{10,11... | collective-permute-start | bytes 9224 | tf_op jit(solution)/shard_map/ppermute | solution.py:30
  53.4 3.7 collective-permute-start.5
  57.2 31.7 %collective-permute-start.6 = (f32[4,2,3,128]{3,2,1,0:T(4,128)S(1)}, f32[4,2,3,128]{3,2,1,0:T(4,128)S(1)}, u32[]{:S(2)}, u32[]{:S(2)}) collective-permute-start(f32[4,2,3,128]{3,2,1,0:T(4,128)S(1)} %bitcast.566), channel_id=1, source_target_pairs={{0,4},{1,5},{2,6},{3,7},{4,0},{5,1},{6,2},{7,3},{8,12},{9,13},{10,... | collective-permute-start | bytes 36872 | tf_op jit(solution)/shard_map/ppermute | solution.py:30
  88.9 4.8 %collective-permute-start.7 = (f32[8,2,3,128]{3,1,0,2:T(2,128)S(1)}, f32[8,2,3,128]{3,1,0,2:T(2,128)S(1)}, u32[]{:S(2)}, u32[]{:S(2)}) collective-permute-start(f32[8,2,3,128]{3,1,0,2:T(2,128)S(1)} %copy.39), channel_id=1, source_target_pairs={{0,8},{1,9},{2,10},{3,11},{4,12},{5,13},{6,14},{7,15},{8,0},{9,1},... | collective-permute-start | bytes 73736 | tf_op jit(solution)/shard_map/ppermute | solution.py:30
  139.0 5.0 %collective-permute-start.10 = (f32[1,2,3,128]{3,2,1,0:T(4,128)S(1)}, f32[1,2,3,128]{3,2,1,0:T(4,128)S(1)}, u32[]{:S(2)}, u32[]{:S(2)}) collective-permute-start(f32[1,2,3,128]{3,2,1,0:T(4,128)S(1)} %bitcast.764), channel_id=1, source_target_pairs={{0,1},{1,0},{2,3},{3,2},{4,5},{5,4},{6,7},{7,6},{8,9},{9,8},{10,11... | collective-permute-start | bytes 9224 | tf_op jit(solution)/shard_map/ppermute | solution.py:30
  139.4 5.8 %collective-permute-start.8 = (f32[3,512]{1,0:T(4,128)S(1)}, f32[3,512]{1,0:T(4,128)S(1)}, u32[]{:S(2)}, u32[]{:S(2)}) collective-permute-start(f32[3,512]{1,0:T(4,128)S(1)} %get-tuple-element.1062), channel_id=1, source_target_pairs={{0,1},{1,2},{2,3},{3,4},{4,5},{5,6},{6,7},{7,8},{8,9},{9,10},{10,1... | collective-permute-start | bytes 18440 | tf_op jit(solution)/shard_map/ppermute | solution.py:44
  139.9 5.5 %collective-permute-start.9 = (f32[3,512]{1,0:T(4,128)S(1)}, f32[3,512]{1,0:T(4,128)S(1)}, u32[]{:S(2)}, u32[]{:S(2)}) collective-permute-start(f32[3,512]{1,0:T(4,128)S(1)} %get-tuple-element.1063), channel_id=1, source_target_pairs={{1,0},{2,1},{3,2},{4,3},{5,4},{6,5},{7,6},{8,7},{9,8},{10,9},{11,1... | collective-permute-start | bytes 18440 | tf_op jit(solution)/shard_map/ppermute | solution.py:46
  144.0 28.8 %collective-permute-start.11 = (f32[2,2,3,128]{3,2,1,0:T(4,128)S(1)}, f32[2,2,3,128]{3,2,1,0:T(4,128)S(1)}, u32[]{:S(2)}, u32[]{:S(2)}) collective-permute-start(f32[2,2,3,128]{3,2,1,0:T(4,128)S(1)} %get-tuple-element.1080), channel_id=1, source_target_pairs={{0,2},{1,3},{2,0},{3,1},{4,6},{5,7},{6,4},{7,5},{8,10},{9,11},{10,... | collective-permute-start | bytes 18440 | tf_op jit(solution)/shard_map/ppermute | solution.py:30
  172.9 4.1 %collective-permute-start.12 = (f32[4,2,3,128]{3,2,1,0:T(4,128)S(1)}, f32[4,2,3,128]{3,2,1,0:T(4,128)S(1)}, u32[]{:S(2)}, u32[]{:S(2)}) collective-permute-start(f32[4,2,3,128]{3,2,1,0:T(4,128)S(1)} %bitcast.570), channel_id=1, source_target_pairs={{0,4},{1,5},{2,6},{3,7},{4,0},{5,1},{6,2},{7,3},{8,12},{9,13},{10,... | collective-permute-start | bytes 36872 | tf_op jit(solution)/shard_map/ppermute | solution.py:30
  177.0 4.8 %collective-permute-start.13 = (f32[8,2,3,128]{3,1,0,2:T(2,128)S(1)}, f32[8,2,3,128]{3,1,0,2:T(2,128)S(1)}, u32[]{:S(2)}, u32[]{:S(2)}) collective-permute-start(f32[8,2,3,128]{3,1,0,2:T(2,128)S(1)} %copy.44), channel_id=1, source_target_pairs={{0,8},{1,9},{2,10},{3,11},{4,12},{5,13},{6,14},{7,15},{8,0},{9,1},... | collective-permute-start | bytes 73736 | tf_op jit(solution)/shard_map/ppermute | solution.py:30
  294.2 5.0 %collective-permute-start.16 = (f32[1,2,3,128]{3,2,1,0:T(4,128)S(1)}, f32[1,2,3,128]{3,2,1,0:T(4,128)S(1)}, u32[]{:S(2)}, u32[]{:S(2)}) collective-permute-start(f32[1,2,3,128]{3,2,1,0:T(4,128)S(1)} %bitcast.762), channel_id=1, source_target_pairs={{0,1},{1,0},{2,3},{3,2},{4,5},{5,4},{6,7},{7,6},{8,9},{9,8},{10,11... | collective-permute-start | bytes 9224 | tf_op jit(solution)/shard_map/ppermute | solution.py:30
  294.6 5.8 %collective-permute-start.14 = (f32[3,512]{1,0:T(4,128)S(1)}, f32[3,512]{1,0:T(4,128)S(1)}, u32[]{:S(2)}, u32[]{:S(2)}) collective-permute-start(f32[3,512]{1,0:T(4,128)S(1)} %get-tuple-element.1054), channel_id=1, source_target_pairs={{0,1},{1,2},{2,3},{3,4},{4,5},{5,6},{6,7},{7,8},{8,9},{9,10},{10,1... | collective-permute-start | bytes 18440 | tf_op jit(solution)/shard_map/ppermute | solution.py:44
  295.1 5.5 %collective-permute-start.15 = (f32[3,512]{1,0:T(4,128)S(1)}, f32[3,512]{1,0:T(4,128)S(1)}, u32[]{:S(2)}, u32[]{:S(2)}) collective-permute-start(f32[3,512]{1,0:T(4,128)S(1)} %get-tuple-element.1055), channel_id=1, source_target_pairs={{1,0},{2,1},{3,2},{4,3},{5,4},{6,5},{7,6},{8,7},{9,8},{10,9},{11,1... | collective-permute-start | bytes 18440 | tf_op jit(solution)/shard_map/ppermute | solution.py:46
  299.3 28.8 %collective-permute-start.17 = (f32[2,2,3,128]{3,2,1,0:T(4,128)S(1)}, f32[2,2,3,128]{3,2,1,0:T(4,128)S(1)}, u32[]{:S(2)}, u32[]{:S(2)}) collective-permute-start(f32[2,2,3,128]{3,2,1,0:T(4,128)S(1)} %get-tuple-element.1078), channel_id=1, source_target_pairs={{0,2},{1,3},{2,0},{3,1},{4,6},{5,7},{6,4},{7,5},{8,10},{9,11},{10,... | collective-permute-start | bytes 18440 | tf_op jit(solution)/shard_map/ppermute | solution.py:30
  328.2 4.1 %collective-permute-start.18 = (f32[4,2,3,128]{3,2,1,0:T(4,128)S(1)}, f32[4,2,3,128]{3,2,1,0:T(4,128)S(1)}, u32[]{:S(2)}, u32[]{:S(2)}) collective-permute-start(f32[4,2,3,128]{3,2,1,0:T(4,128)S(1)} %bitcast.568), channel_id=1, source_target_pairs={{0,4},{1,5},{2,6},{3,7},{4,0},{5,1},{6,2},{7,3},{8,12},{9,13},{10,... | collective-permute-start | bytes 36872 | tf_op jit(solution)/shard_map/ppermute | solution.py:30
  332.3 4.8 %collective-permute-start.19 = (f32[8,2,3,128]{3,1,0,2:T(2,128)S(1)}, f32[8,2,3,128]{3,1,0,2:T(2,128)S(1)}, u32[]{:S(2)}, u32[]{:S(2)}) collective-permute-start(f32[8,2,3,128]{3,1,0,2:T(2,128)S(1)} %copy.49), channel_id=1, source_target_pairs={{0,8},{1,9},{2,10},{3,11},{4,12},{5,13},{6,14},{7,15},{8,0},{9,1},... | collective-permute-start | bytes 73736 | tf_op jit(solution)/shard_map/ppermute | solution.py:30
  (8 other events, 50.9 us)
